TPU v7x, 32 devices: a whole 2x2x4 slice. The times are simulated.
32 devices in a mesh: tok: 16 (over z, x, core), col: 2 (over y).
Axes of the slice: x: 2, y: 2, z: 4, core: 2. Of those that a mesh axis runs over, the one named last changes fastest.
Arguments:
- tokens: bfloat16 [12288, 2048], P('tok', 'col'), may hold values from -6 to 6
- cotangent: bfloat16 [12288, 2048], P('tok', 'col'), may hold values from -6 to 6
- query_weight: bfloat16 [2048, 2048], P(None, 'col'), may hold values from -1 to 1
- slot_keys: bfloat16 [16384, 2048], P('tok', 'col'), may hold values from -64 to 64
- values: float32 [16384, 2048], P('tok', 'col'), may hold values from -6 to 6
- momentum: float32 [16384, 2048], P('tok', 'col'), may hold values from -0.3 to 0.3
- page_ids: int32 [192, 4], P('tok'), may hold values from 0 to 127, as said below
- last_step: int32 [128], P('tok'), may hold values from 0 to 63
- decay_rate: float32 [2048], P('col'), may hold values from 0.004 to 0.08
- gate_weight: bfloat16 [2048, 2048], P(None, 'col'), may hold values from -0.125 to 0.125
- out_weight: bfloat16 [2048, 2048], P('col'), may hold values from -0.1875 to 0.1875
Outputs:
- layer_out: bfloat16 [12288, 2048], P('tok', 'col')
- new_values: float32 [16384, 2048], P('tok', 'col')
- new_momentum: float32 [16384, 2048], P('tok', 'col')
Inputs may be any that keep to these rules, and one draw needn't show every extreme that they name: `page_ids`: page p belongs to owner group p // 8. Among the 48 pages listed by the blocks of one index of tok, counted with repeats, at most 4 belong to any one owner group, and one owner group gets exactly 4 from every index of tok. A block may list a page more than once.
All inputs are finite; a program needn't handle non-finite values.
Results may differ from a plain program's by a relative error of at most 0.014.
Values may be sent and summed in bfloat16 or wider, within the bound.
No kernel may reach another device: no remote copies, remote signals or barrier semaphores. Data moves between devices by JAX's collectives and lax.ppermute only.
A program may use at most 128 MiB of HBM per device.

v0:
```python
import jax
import jax.numpy as jnp
from jax import lax
from jax.sharding import PartitionSpec as P

KW = 2048
STEP = 64
MOMENTUM_RATE = 0.9
LEARN_RATE = 1.0


def per_device(
    tokens,
    cotangent,
    query_weight,
    slot_keys,
    values,
    momentum,
    page_ids,
    last_step,
    decay_rate,
    gate_weight,
    out_weight,
):
    tok_rows = tokens.shape[0]
    col_width = values.shape[1]
    key_width = slot_keys.shape[1]
    block_count, per_block = page_ids.shape
    block_rows = tok_rows // block_count
    pages_local = last_step.shape[0]
    page_slots = values.shape[0] // pages_local
    owners = lax.axis_size("tok")
    capacity = max(2, per_block * block_count // owners + 1)
    send_slots = owners * capacity
    listed_slots = per_block * page_slots
    elapsed = (STEP - last_step).astype(jnp.float32)
    factor = jnp.exp(-elapsed[:, None] * decay_rate[None, :])
    stored = values.reshape(pages_local, page_slots, col_width)
    decayed = (stored * factor[:, None, :]).astype(jnp.bfloat16)
    key_pages = slot_keys.reshape(pages_local, page_slots, key_width)
    token_piece = lax.all_gather(tokens, "col", axis=1, tiled=True)
    cotangent_piece = lax.all_gather(cotangent, "col", axis=1, tiled=True)
    query_sum = jnp.dot(token_piece, query_weight, preferred_element_type=jnp.float32)
    gate_logits = jnp.dot(token_piece, gate_weight, preferred_element_type=jnp.float32)
    grad_gated = jnp.einsum(
        "nd,cd->nc", cotangent_piece, out_weight, preferred_element_type=jnp.float32
    )
    requested = page_ids.reshape(-1)
    page_owner = requested // pages_local
    local_page = requested % pages_local
    request_count = requested.shape[0]
    positions = jnp.arange(request_count)
    same_owner = page_owner[:, None] == page_owner[None, :]
    slot_rank = jnp.sum(same_owner & (positions[None, :] < positions[:, None]), axis=1)
    send_slot = page_owner * capacity + slot_rank
    slot_match = send_slot[:, None] == jnp.arange(send_slots)[None, :]
    wanted = jnp.sum(jnp.where(slot_match, local_page[:, None] + 1, 0), axis=0) - 1
    wanted = wanted.reshape(owners, capacity)
    incoming = lax.all_to_all(wanted, "tok", split_axis=0, concat_axis=0, tiled=True)
    occupied = (incoming >= 0)[:, :, None, None]
    chosen = jnp.clip(incoming, 0, pages_local - 1)
    reply_keys = jnp.where(occupied, key_pages[chosen], jnp.zeros((), jnp.bfloat16))
    reply_values = jnp.where(occupied, decayed[chosen], jnp.zeros((), jnp.bfloat16))
    got_keys = lax.all_to_all(reply_keys, "tok", split_axis=0, concat_axis=0, tiled=True)
    got_values = lax.all_to_all(reply_values, "tok", split_axis=0, concat_axis=0, tiled=True)
    block_keys = got_keys.reshape(send_slots, page_slots, key_width)[send_slot]
    block_keys = block_keys.reshape(block_count, listed_slots, key_width)
    block_values = got_values.reshape(send_slots, page_slots, col_width)[send_slot]
    block_values = block_values.reshape(block_count, listed_slots, col_width)
    queries = query_sum.astype(jnp.bfloat16).reshape(block_count, block_rows, key_width)
    partial_scores = jnp.einsum(
        "bnk,bsk->bns", queries, block_keys, preferred_element_type=jnp.float32
    )
    score_scale = KW ** (-0.5)
    flat_scores = partial_scores.reshape(tok_rows, listed_slots)
    score_share = (
        lax.psum_scatter(flat_scores, "col", scatter_dimension=0, tiled=True) * score_scale
    )
    share_weights = jax.nn.softmax(score_share, axis=-1).astype(jnp.bfloat16)
    weights = lax.all_gather(share_weights, "col", axis=0, tiled=True).reshape(
        block_count, block_rows, listed_slots
    )
    memory = jnp.einsum("bns,bsd->bnd", weights, block_values, preferred_element_type=jnp.float32)
    memory = memory.reshape(tok_rows, col_width)
    activation = jax.nn.silu(gate_logits)
    gated_memory = (memory * activation).astype(jnp.bfloat16)
    out_terms = jnp.dot(gated_memory, out_weight, preferred_element_type=jnp.float32)
    layer_out = lax.psum_scatter(
        out_terms.astype(jnp.bfloat16), "col", scatter_dimension=1, tiled=True
    )
    grad_memory = (
        (grad_gated * activation).astype(jnp.bfloat16).reshape(block_count, block_rows, col_width)
    )
    slot_grads = jnp.einsum(
        "bns,bnd->bsd", weights, grad_memory, preferred_element_type=jnp.float32
    ).astype(jnp.bfloat16)
    outgoing = jnp.zeros((send_slots, page_slots, col_width), jnp.bfloat16)
    outgoing = outgoing.at[send_slot].set(slot_grads.reshape(request_count, page_slots, col_width))
    returned = lax.all_to_all(
        outgoing.reshape(owners, capacity, page_slots, col_width),
        "tok",
        split_axis=0,
        concat_axis=0,
        tiled=True,
    )
    page_match = incoming.reshape(1, send_slots) == jnp.arange(pages_local)[:, None]
    page_grad = jnp.dot(
        page_match.astype(jnp.bfloat16),
        returned.reshape(send_slots, page_slots * col_width),
        preferred_element_type=jnp.float32,
    )
    page_grad = page_grad.reshape(pages_local, page_slots, col_width)
    touched = jnp.any(page_match, axis=1)[:, None, None]
    moment = momentum.reshape(pages_local, page_slots, col_width)
    new_momentum = jnp.where(
        touched, MOMENTUM_RATE * moment + page_grad * factor[:, None, :], moment
    )
    new_values = jnp.where(touched, stored * factor[:, None, :] - LEARN_RATE * new_momentum, stored)
    return (layer_out, new_values.reshape(-1, col_width), new_momentum.reshape(-1, col_width))


def solution(mesh):
    in_specs = (
        P("tok", "col"),
        P("tok", "col"),
        P(None, "col"),
        P("tok", "col"),
        P("tok", "col"),
        P("tok", "col"),
        P("tok", None),
        P("tok"),
        P("col"),
        P(None, "col"),
        P("col", None),
    )
    out_specs = (P("tok", "col"), P("tok", "col"), P("tok", "col"))
    return jax.shard_map(
        per_device, mesh=mesh, in_specs=in_specs, out_specs=out_specs, check_vma=False
    )
```

profile of v0, /device:TPU:0, one launch (start us, length us, event | category | flops | bytes accessed | tf_op | source)
XLA Modules:
  0.0 1397.6 jit_solution(13270048119418362849)
XLA Ops:
  8.6 13.6 all_to_all.21
  22.6 7.5 gather_fusion
  30.1 14.0 %broadcast_select_fusion.1 = bf16[16,4,128,1024]{3,2,1,0:T(8,128)(2,1)} fusion(bf16[16,4,128,1024]{3,2,1,0:T(8,128)(2,1)} %bitcast.73, pred[16,4]{1,0:T(8,128)(4,1)S(1)} %copy.68), kind=kLoop, calls=%fused_computation.9 | loop fusion | flops 8388608 | bytes 33554496 | tf_op jit(solution)/shard_map/jit(_where)/select_n | solution.py:62
  44.0 5.2 all-to-all-start.1
  50.9 46.9 %all-gather.3.cloned.1.call-done = bf16[768,2048]{1,0:T(8,128)(2,1)} async-done(((bf16[768,1024]{1,0:T(8,128)(2,1)}), bf16[768,2048]{1,0:T(8,128)(2,1)}) %all-gather.3.cloned.1.call-update) | async-done | bytes 3145744 | tf_op jit(solution)/shard_map/all_gather | solution.py:41
  97.7 6.6 convolution_convert_fusion.2
  104.3 241.5 %all-to-all-done.1 = bf16[16,4,128,1024]{3,2,1,0:T(8,128)(2,1)} async-done(((bf16[16,4,128,1024]{3,2,1,0:T(8,128)(2,1)}), bf16[16,4,128,1024]{3,2,1,0:T(8,128)(2,1)}, u32[]{:S(2)}, u32[]{:S(2)}) %all-to-all-start.1) | async-done | bytes 16777248 | tf_op jit(solution)/shard_map/all_to_all | solution.py:64
  345.8 12.1 gather_fusion.1
  357.9 9.6 fusion.15
  367.6 8.2 fusion.17
  375.8 7.7 multiply_convert_fusion
  383.5 75.9 %reduce-scatter.3.cloned.1.call-done = f32[384,512]{1,0:T(8,128)} async-done(((f32[768,512]{1,0:T(8,128)}), f32[384,512]{1,0:T(8,128)}) %reduce-scatter.3.cloned.1.call-update) | async-done | bytes 786448 | tf_op jit(solution)/shard_map/reduce_scatter | solution.py:77
  459.4 1.3 multiply_reduce_fusion
  460.7 1.4 fusion.7
  462.1 1.4 divide_convert_fusion
  463.5 24.0 %all_gather.10 = bf16[768,512]{1,0:T(8,128)(2,1)S(1)} all-gather(bf16[384,512]{1,0:T(8,128)(2,1)S(1)} %divide_convert_fusion), channel_id=1, replica_groups=mesh['tok'=16,'col'=2] {'col'}, dimensions={0}, use_global_device_ids=true | all-gather | bytes 1179648 | tf_op jit(solution)/shard_map/all_gather | solution.py:80
  487.5 6.4 convolution_convert_fusion
  493.9 6.0 broadcast_in_dim.69
  499.9 31.7 %scatter_fusion = bf16[64,128,1024]{2,1,0:T(8,128)(2,1)} fusion(bf16[64,128,1024]{2,1,0:T(8,128)(2,1)} %broadcast_in_dim.69, s32[48]{0:T(128)S(1)} %fusion.14, bf16[48,128,1024]{2,1,0:T(8,128)(2,1)} %bitcast.75), kind=kCustom, calls=%fused_computation.4 | custom fusion | bytes 37748928 | tf_op jit(solution)/shard_map/scatter | solution.py:98
  531.6 6.1 all-to-all-start.3
  539.2 295.1 %all-to-all-done.3 = bf16[16,4,128,1024]{3,2,1,0:T(8,128)(2,1)} async-done(((bf16[16,4,128,1024]{3,2,1,0:T(8,128)(2,1)}), bf16[16,4,128,1024]{3,2,1,0:T(8,128)(2,1)}, u32[]{:S(2)}, u32[]{:S(2)}) %all-to-all-start.3) | async-done | bytes 16777248 | tf_op jit(solution)/shard_map/all_to_all | solution.py:99
  834.3 36.8 %subtract_select_fusion = (f32[8,128,1024]{2,0,1:T(8,128)}, bf16[8,128,1024]{2,0,1:T(8,128)(2,1)S(1)}, f32[8,128,1024]{2,0,1:T(8,128)}) fusion(f32[8,128,1024]{2,1,0:T(8,128)} %bitcast.80, f32[8,1024]{1,0:T(8,128)S(1)} %multiply_exponential_fusion, pred[8]{0:T(512)(128)(4,1)S(1)} %fusion.10, s32[64]{0:T(128)S(1)} %eq.49, f32[8,128,1024]{2,1,0:T(8,128)} %bitcast.81, ...), kind=kOutput, calls=%fused_computation.11 | convolution fusion | flops 142606848 | bytes 35684616 | tf_op jit(solution)/shard_map/dot_general | solution.py:107
  871.1 1.2 copy.73
  872.3 7.5 gather_fusion.2
  879.7 8.3 broadcast_select_fusion
  888.0 431.9 %all_to_all.22 = bf16[16,4,128,1024]{3,2,1,0:T(8,128)(2,1)} all-to-all(bf16[16,4,128,1024]{3,2,1,0:T(8,128)(2,1)S(1)} %broadcast_select_fusion), channel_id=1, replica_groups=mesh['tok'=16,'col'=2] {'tok'}, dimensions={0} | all-to-all | bytes 33554432 | tf_op jit(solution)/shard_map/all_to_all | solution.py:65
  1319.9 12.1 gather_fusion.3
  1332.0 7.0 fusion.16
  1341.2 4.8 convolution_convert_fusion.1
  1346.1 6.8 copy.78
  1352.9 4.4 copy.79
  1357.3 33.3 %reduce-scatter.5.cloned.1.call-done = bf16[768,1024]{1,0:T(8,128)(2,1)} async-done(((bf16[768,2048]{1,0:T(8,128)(2,1)}), bf16[768,1024]{1,0:T(8,128)(2,1)}) %reduce-scatter.5.cloned.1.call-update) | async-done | bytes 1572880 | tf_op jit(solution)/shard_map/reduce_scatter | solution.py:88
  (48 shorter events, 7.1 us)
Async XLA Ops:
  7.2 15.4 %copy-start = (bf16[1024,1024]{1,0:T(8,128)(2,1)S(1)}, bf16[1024,1024]{1,0:T(8,128)(2,1)}, u32[]{:S(2)}) copy-start(bf16[1024,1024]{1,0:T(8,128)(2,1)} %param.14) | copy-start | bytes 6291460
  44.0 301.7 %all-to-all-start.1 = ((bf16[16,4,128,1024]{3,2,1,0:T(8,128)(2,1)}), bf16[16,4,128,1024]{3,2,1,0:T(8,128)(2,1)}, u32[]{:S(2)}, u32[]{:S(2)}) async-start(bf16[16,4,128,1024]{3,2,1,0:T(8,128)(2,1)} %broadcast_select_fusion.1), calls=%async_computation.1 | async-start | bytes 33554432 | tf_op jit(solution)/shard_map/all_to_all | solution.py:64
  49.2 48.5 %all-gather.3.cloned.1.call-start = ((), (), s32[]{:S(2)}) async-start(), calls=%async_computation.6 | async-start | bytes 4718592 | tf_op jit(solution)/shard_map/all_gather | solution.py:41
  49.9 325.9 %all-gather.5.cloned.1.call-start = ((), (), s32[]{:S(2)}) async-start(), calls=%async_computation.9 | async-start | bytes 4718592 | tf_op jit(solution)/shard_map/all_gather | solution.py:42
  50.7 408.7 %reduce-scatter.3.cloned.1.call-start = ((), (), s32[]{:S(2)}) async-start(), calls=%async_computation.7 | async-start | bytes 2359296 | tf_op jit(solution)/shard_map/reduce_scatter | solution.py:77
  531.6 6.1 copy-start.6
  531.6 6.2 copy-start.4
  531.6 302.7 %all-to-all-start.3 = ((bf16[16,4,128,1024]{3,2,1,0:T(8,128)(2,1)}), bf16[16,4,128,1024]{3,2,1,0:T(8,128)(2,1)}, u32[]{:S(2)}, u32[]{:S(2)}) async-start(bf16[16,4,128,1024]{3,2,1,0:T(8,128)(2,1)} %bitcast.70), calls=%async_computation.5 | async-start | bytes 33554432 | tf_op jit(solution)/shard_map/all_to_all | solution.py:99
  537.7 853.0 %reduce-scatter.5.cloned.1.call-start = ((), (), s32[]{:S(2)}) async-start(), calls=%async_computation.8 | async-start | bytes 4718592 | tf_op jit(solution)/shard_map/reduce_scatter | solution.py:88
  1332.0 7.0 copy-start.3
  1339.1 2.2 copy-start.5
  1346.1 6.8 copy-start.2
  1352.9 37.8 %copy-start.1 = (bf16[1024,1024]{1,0:T(8,128)(2,1)S(1)}, bf16[1024,1024]{1,0:T(8,128)(2,1)}, u32[]{:S(2)}) copy-start(bf16[1024,1024]{1,0:T(8,128)(2,1)} %param.14) | copy-start | bytes 6291460
Sparse Core Ops, SparseCore 0:
  51.6 46.1 all-gather.2
  99.3 44.8 all-gather.4
  367.7 91.6 reduce-scatter.2
  1346.2 44.3 reduce-scatter.4
where the time goes:
time: 1410 us; the launch traced here: 1400 us
  waiting for transfers between devices  694 us (49%)
  blocking collectives  469 us (33%)
  local copies, waits for them, and re-layouts  92.6 us (7%)
  matrix products  87.2 us (6%)
  other arithmetic  28.6 us (2%)
  between operations  14.3 us (1%)
    all_to_all x1, blocking collectives, per_device(): lax.all_to_all(reply_values, 'tok', split_axis=0, concat_axis=0, tiled=True)  432 us
    all_to_all x1, waiting for transfers between devices, per_device(): lax.all_to_all(outgoing.reshape(owners, capacity, page_slots, col_width),...  295 us
    all_to_all x1, waiting for transfers between devices, per_device(): lax.all_to_all(reply_keys, 'tok', split_axis=0, concat_axis=0, tiled=True)  241 us
    reduce_scatter x1, waiting for transfers between devices, per_device(): lax.psum_scatter(flat_scores, 'col', scatter_dimension=0, tiled=True)  75.9 us
    all_gather x1, waiting for transfers between devices, per_device(): token_piece = lax.all_gather(tokens, 'col', axis=1, tiled=True)  46.9 us
    dot_general x1, matrix products, per_device(): jnp.dot(page_match.astype(jnp.bfloat16), returned.reshape(send_slots, pag...  36.8 us
    reduce_scatter x1, waiting for transfers between devices, per_device(): lax.psum_scatter(out_terms.astype(jnp.bfloat16), 'col', scatter_dimension...  33.3 us
    scatter x1, local copies, waits for them, and re-layouts, per_device(): outgoing.at[send_slot]  31.7 us
  transfers between devices with their start and end apart: 6, of which 5 were waited for; matrix products, arithmetic and copies ran while one was open for 4% of the time, Pallas kernels for 0%

commit v1 on v0

--- a/solution.py
+++ b/solution.py
@@ -38,8 +38,11 @@
     stored = values.reshape(pages_local, page_slots, col_width)
     decayed = (stored * factor[:, None, :]).astype(jnp.bfloat16)
     key_pages = slot_keys.reshape(pages_local, page_slots, key_width)
-    token_piece = lax.all_gather(tokens, "col", axis=1, tiled=True)
-    cotangent_piece = lax.all_gather(cotangent, "col", axis=1, tiled=True)
+    token_piece, cotangent_piece = jnp.split(
+        lax.all_gather(jnp.concatenate([tokens, cotangent], axis=0), "col", axis=1, tiled=True),
+        [tokens.shape[0]],
+        axis=0,
+    )
     query_sum = jnp.dot(token_piece, query_weight, preferred_element_type=jnp.float32)
     gate_logits = jnp.dot(token_piece, gate_weight, preferred_element_type=jnp.float32)
     grad_gated = jnp.einsum(

time: 1410 us -> 1400 us (level)
    all_to_all x1, waiting for transfers between devices: 241 us -> 205 us  [per_device(): lax.all_to_all(reply_keys, 'tok', split_axis=0, concat_axis=0, tiled=True)]
    all_gather x2 -> x1, waiting for transfers between devices: 46.9 us -> 81.2 us  [per_device(): lax.all_gather(jnp.concatenate([tokens, cotangent], axis=0), 'col', axis=...]
  transfers between devices with their start and end apart: 6 -> 5, of which waited for: 5 -> 5; matrix products, arithmetic and copies ran while one was open for 4% -> 2% of each run, Pallas kernels for 0% -> 0%
where the time goes in v1:
time: 1400 us
  waiting for transfers between devices  692 us (49%)
  blocking collectives  457 us (33%)
  local copies, waits for them, and re-layouts  94.5 us (7%)
  matrix products  94.2 us (7%)
  other arithmetic  31.7 us (2%)
  between operations  14.2 us (1%)
    all_to_all x1, blocking collectives, per_device(): lax.all_to_all(reply_values, 'tok', split_axis=0, concat_axis=0, tiled=True)  432 us
    all_to_all x1, waiting for transfers between devices, per_device(): lax.all_to_all(outgoing.reshape(owners, capacity, page_slots, col_width),...  295 us
    all_to_all x1, waiting for transfers between devices, per_device(): lax.all_to_all(reply_keys, 'tok', split_axis=0, concat_axis=0, tiled=True)  205 us
    all_gather x1, waiting for transfers between devices, per_device(): lax.all_gather(jnp.concatenate([tokens, cotangent], axis=0), 'col', axis=...  81.2 us
    reduce_scatter x1, waiting for transfers between devices, per_device(): lax.psum_scatter(flat_scores, 'col', scatter_dimension=0, tiled=True)  78.1 us
    dot_general x1, matrix products, per_device(): jnp.dot(page_match.astype(jnp.bfloat16), returned.reshape(send_slots, pag...  47.7 us
    reduce_scatter x1, waiting for transfers between devices, per_device(): lax.psum_scatter(out_terms.astype(jnp.bfloat16), 'col', scatter_dimension...  33.3 us
    scatter x1, local copies, waits for them, and re-layouts, per_device(): outgoing.at[send_slot]  31.7 us
  transfers between devices with their start and end apart: 5, of which 5 were waited for; matrix products, arithmetic and copies ran while one was open for 2% of the time, Pallas kernels for 0%

profile of v1, /device:TPU:0, one launch (start us, length us, event | category | flops | bytes accessed | tf_op | source)
XLA Modules:
  0.0 1395.8 jit_solution(2636985975134296763)
XLA Ops:
  8.6 13.6 all_to_all.21
  22.6 7.5 gather_fusion
  30.1 14.0 %broadcast_select_fusion.1 = bf16[16,4,128,1024]{3,2,1,0:T(8,128)(2,1)} fusion(bf16[16,4,128,1024]{3,2,1,0:T(8,128)(2,1)} %bitcast.70, pred[16,4]{1,0:T(8,128)(4,1)S(1)} %copy.68), kind=kLoop, calls=%fused_computation.9 | loop fusion | flops 8388608 | bytes 33554496 | tf_op jit(solution)/shard_map/jit(_where)/select_n | solution.py:65
  44.0 5.3 all-to-all-start.1
  49.4 3.4 pad_maximum_fusion
  53.3 81.2 %all-gather.2.cloned.1.call-done = bf16[1536,2048]{1,0:T(8,128)(2,1)} async-done(((bf16[1536,1024]{1,0:T(8,128)(2,1)}), bf16[1536,2048]{1,0:T(8,128)(2,1)}) %all-gather.2.cloned.1.call-update) | async-done | bytes 6291472 | tf_op jit(solution)/shard_map/all_gather | solution.py:42
  134.6 6.6 fusion.17
  141.1 204.8 %all-to-all-done.1 = bf16[16,4,128,1024]{3,2,1,0:T(8,128)(2,1)} async-done(((bf16[16,4,128,1024]{3,2,1,0:T(8,128)(2,1)}), bf16[16,4,128,1024]{3,2,1,0:T(8,128)(2,1)}, u32[]{:S(2)}, u32[]{:S(2)}) %all-to-all-start.1) | async-done | bytes 16777248 | tf_op jit(solution)/shard_map/all_to_all | solution.py:67
  345.9 12.1 gather_fusion.1
  358.0 9.6 fusion.28
  367.7 6.7 divide_multiply_fusion
  374.5 1.7 copy-done.3
  376.1 5.4 multiply_convert_fusion
  381.5 78.1 %reduce-scatter.3.cloned.1.call-done = f32[384,512]{1,0:T(8,128)} async-done(((f32[768,512]{1,0:T(8,128)}), f32[384,512]{1,0:T(8,128)}) %reduce-scatter.3.cloned.1.call-update) | async-done | bytes 786448 | tf_op jit(solution)/shard_map/reduce_scatter | solution.py:80
  460.9 1.4 fusion.20
  463.6 11.4 all_gather.7
  475.0 6.4 convolution_convert_fusion
  481.4 6.0 broadcast_in_dim.69
  487.4 31.7 %scatter_fusion = bf16[64,128,1024]{2,1,0:T(8,128)(2,1)} fusion(bf16[64,128,1024]{2,1,0:T(8,128)(2,1)} %broadcast_in_dim.69, s32[48]{0:T(128)S(1)} %fusion.27, bf16[48,128,1024]{2,1,0:T(8,128)(2,1)} %bitcast.72), kind=kCustom, calls=%fused_computation.4 | custom fusion | bytes 37748928 | tf_op jit(solution)/shard_map/scatter | solution.py:101
  519.1 6.0 all-to-all-start.3
  526.7 295.1 %all-to-all-done.3 = bf16[16,4,128,1024]{3,2,1,0:T(8,128)(2,1)} async-done(((bf16[16,4,128,1024]{3,2,1,0:T(8,128)(2,1)}), bf16[16,4,128,1024]{3,2,1,0:T(8,128)(2,1)}, u32[]{:S(2)}, u32[]{:S(2)}) %all-to-all-start.3) | async-done | bytes 16777248 | tf_op jit(solution)/shard_map/all_to_all | solution.py:102
  821.8 47.7 %subtract_select_fusion = (f32[8,128,1024]{2,0,1:T(8,128)}, bf16[8,128,1024]{2,0,1:T(8,128)(2,1)S(1)}, f32[8,128,1024]{2,0,1:T(8,128)}) fusion(f32[8,128,1024]{2,1,0:T(8,128)} %bitcast.77, f32[8,1024]{1,0:T(8,128)S(1)} %multiply_exponential_fusion, pred[8]{0:T(512)(128)(4,1)S(1)} %fusion.23, s32[64]{0:T(128)S(1)} %eq.49, f32[8,128,1024]{2,1,0:T(8,128)} %bitcast.78, ...), kind=kOutput, calls=%fused_computation.11 | convolution fusion | flops 142606848 | bytes 35684616 | tf_op jit(solution)/shard_map/dot_general | solution.py:110
  870.6 7.5 gather_fusion.2
  878.1 8.3 broadcast_select_fusion
  886.4 431.9 %all_to_all.22 = bf16[16,4,128,1024]{3,2,1,0:T(8,128)(2,1)} all-to-all(bf16[16,4,128,1024]{3,2,1,0:T(8,128)(2,1)S(1)} %broadcast_select_fusion), channel_id=1, replica_groups=mesh['tok'=16,'col'=2] {'tok'}, dimensions={0} | all-to-all | bytes 33554432 | tf_op jit(solution)/shard_map/all_to_all | solution.py:68
  1318.3 12.1 gather_fusion.3
  1330.4 7.0 fusion.29
  1338.2 1.4 copy-done.8
  1339.6 4.8 convolution_convert_fusion.1
  1344.5 6.8 copy.78
  1351.3 4.4 copy.79
  1355.7 33.3 %reduce-scatter.5.cloned.1.call-done = bf16[768,1024]{1,0:T(8,128)(2,1)} async-done(((bf16[768,2048]{1,0:T(8,128)(2,1)}), bf16[768,1024]{1,0:T(8,128)(2,1)}) %reduce-scatter.5.cloned.1.call-update) | async-done | bytes 1572880 | tf_op jit(solution)/shard_map/reduce_scatter | solution.py:91
  (52 shorter events, 8.5 us)
Async XLA Ops:
  7.2 15.4 %copy-start = (bf16[1024,1024]{1,0:T(8,128)(2,1)S(1)}, bf16[1024,1024]{1,0:T(8,128)(2,1)}, u32[]{:S(2)}) copy-start(bf16[1024,1024]{1,0:T(8,128)(2,1)} %param.14) | copy-start | bytes 6291460
  44.0 5.3 copy-start.5
  44.0 301.9 %all-to-all-start.1 = ((bf16[16,4,128,1024]{3,2,1,0:T(8,128)(2,1)}), bf16[16,4,128,1024]{3,2,1,0:T(8,128)(2,1)}, u32[]{:S(2)}, u32[]{:S(2)}) async-start(bf16[16,4,128,1024]{3,2,1,0:T(8,128)(2,1)} %broadcast_select_fusion.1), calls=%async_computation.1 | async-start | bytes 33554432 | tf_op jit(solution)/shard_map/all_to_all | solution.py:67
  49.3 85.2 %all-gather.2.cloned.1.call-start = ((), (), s32[]{:S(2)}) async-start(), calls=%async_computation.6 | async-start | bytes 9437184 | tf_op jit(solution)/shard_map/all_gather | solution.py:42
  52.8 406.8 %reduce-scatter.3.cloned.1.call-start = ((), (), s32[]{:S(2)}) async-start(), calls=%async_computation.7 | async-start | bytes 2359296 | tf_op jit(solution)/shard_map/reduce_scatter | solution.py:80
  367.7 8.4 copy-start.7
  374.5 1.7 copy-start.3
  519.1 6.1 copy-start.9
  519.1 6.1 copy-start.6
  519.1 302.7 %all-to-all-start.3 = ((bf16[16,4,128,1024]{3,2,1,0:T(8,128)(2,1)}), bf16[16,4,128,1024]{3,2,1,0:T(8,128)(2,1)}, u32[]{:S(2)}, u32[]{:S(2)}) async-start(bf16[16,4,128,1024]{3,2,1,0:T(8,128)(2,1)} %bitcast.67), calls=%async_computation.5 | async-start | bytes 33554432 | tf_op jit(solution)/shard_map/all_to_all | solution.py:102
  525.2 863.8 %reduce-scatter.5.cloned.1.call-start = ((), (), s32[]{:S(2)}) async-start(), calls=%async_computation.8 | async-start | bytes 4718592 | tf_op jit(solution)/shard_map/reduce_scatter | solution.py:91
  1330.4 7.0 copy-start.4
  1337.4 2.2 copy-start.8
  1344.5 6.8 copy-start.2
  1351.3 37.7 %copy-start.1 = (bf16[1024,1024]{1,0:T(8,128)(2,1)S(1)}, bf16[1024,1024]{1,0:T(8,128)(2,1)}, u32[]{:S(2)}) copy-start(bf16[1024,1024]{1,0:T(8,128)(2,1)} %param.14) | copy-start | bytes 6291460
Sparse Core Ops, SparseCore 0:
  52.9 81.5 all-gather.1
  367.8 91.7 reduce-scatter.2
  1344.6 44.3 reduce-scatter.4
